TPU v7x, 32 devices: a whole 2x2x4 slice. The times are simulated.
32 devices in a mesh: dp: 4 (over y, x), depth: 4 (over z), grid: 2 (over core).
Axes of the slice: x: 2, y: 2, z: 4, core: 2. Of those that a mesh axis runs over, the one named last changes fastest.
Arguments:
- tokens: bfloat16 [1024, 12288], P(('dp', 'depth'), 'grid'), may hold values from -6 to 6
- weight: bfloat16 [12288, 24576], P('grid', 'depth'), may hold values from -0.0546875 to 0.0546875
- cotangent: bfloat16 [1024, 24576], P(('dp', 'grid'), 'depth'), may hold values from -0.5 to 0.5
Outputs:
- hidden: bfloat16 [1024, 24576], P(('dp', 'grid'), 'depth')
- weight_grad: bfloat16 [12288, 24576], P(('grid', 'dp'), 'depth')
All inputs are finite; a program needn't handle non-finite values.
Results may differ from a plain program's by a relative error of at most 0.011.
Values may be sent and summed in bfloat16 or wider, within the bound.
No kernel may reach another device: no remote copies, remote signals or barrier semaphores. Data moves between devices by JAX's collectives and lax.ppermute only.
A program may use at most 192 MiB of HBM per device.

v0:
```python
import jax
import jax.numpy as jnp
from jax import lax
from jax.sharding import PartitionSpec as P


def gelu_tanh(values):
    return jax.nn.gelu(values, approximate=True)


def transposed_product(left, right):
    return lax.dot_general(
        left, right, (((0,), (0,)), ((), ())), preferred_element_type=jnp.float32
    )


def local(tokens, weight, cotangent):
    all_rows = lax.all_gather(tokens, ("dp", "depth"), axis=0, tiled=True)
    group_size = all_rows.shape[0] // lax.axis_size("dp")
    own_rows = lax.dynamic_slice_in_dim(all_rows, lax.axis_index("dp") * group_size, group_size, 0)
    partial_pre = jnp.dot(own_rows, weight, preferred_element_type=jnp.float32)
    preact = lax.psum_scatter(partial_pre, "grid", scatter_dimension=0, tiled=True)
    activated, pullback = jax.vjp(gelu_tanh, preact)
    hidden = activated.astype(jnp.bfloat16)
    grad_pre = pullback(cotangent.astype(jnp.float32))[0].astype(jnp.bfloat16)
    sub_width = all_rows.shape[1] // lax.axis_size("dp")
    columns = lax.dynamic_slice_in_dim(all_rows, lax.axis_index("dp") * sub_width, sub_width, 1)
    weight_grad = transposed_product(
        columns, lax.all_gather(grad_pre, ("dp", "grid"), axis=0, tiled=True)
    )
    return (hidden, weight_grad.astype(jnp.bfloat16))


def solution(mesh):
    return jax.shard_map(
        local,
        mesh=mesh,
        in_specs=(P(("dp", "depth"), "grid"), P("grid", "depth"), P(("dp", "grid"), "depth")),
        out_specs=(P(("dp", "grid"), "depth"), P(("grid", "dp"), "depth")),
        check_vma=False,
    )
```

profile of v0, /device:TPU:0, one launch (start us, length us, event | category | flops | bytes accessed | tf_op | source)
XLA Modules:
  0.0 322.6 jit_solution(14169711380635420403)
XLA Ops:
  7.2 0.0 all-gather.3.cloned.1.call-start
  7.2 0.7 all-gather.3.cloned.1.call-update
  7.9 0.0 reduce-scatter.2.cloned.1.call-start
  7.9 157.1 %all-gather.3.cloned.1.call-done = bf16[1024,6144]{1,0:T(8,128)(2,1)} async-done(((bf16[64,6144]{1,0:T(8,128)(2,1)}), bf16[1024,6144]{1,0:T(8,128)(2,1)}) %all-gather.3.cloned.1.call-update) | async-done | bytes 12582928 | tf_op jit(solution)/shard_map/all_gather | solution.py:18
  165.0 31.6 %fusion.11 = f32[256,6144]{1,0:T(8,128)} fusion(bf16[6144,6144]{1,0:T(8,128)(2,1)} %param.4, bf16[1024,6144]{1,0:T(8,128)(2,1)} %all-gather.3.cloned.1.call-done, s32[]{:T(128)S(6)} %select_n.6), kind=kOutput, calls=%fused_computation.17 | convolution fusion | flops 19327352832 | bytes 84934656 | tf_op jit(solution)/shard_map/dot_general | solution.py:21
  196.6 0.0 copy-start
  196.6 0.0 reduce-scatter.2.cloned.1.call-update
  196.6 0.0 all-gather.5.cloned.1.call-start
  196.7 12.3 %reduce-scatter.2.cloned.1.call-done = f32[128,6144]{1,0:T(8,128)} async-done(((f32[256,6144]{1,0:T(8,128)}), f32[128,6144]{1,0:T(8,128)}) %reduce-scatter.2.cloned.1.call-update) | async-done | bytes 3145744 | tf_op jit(solution)/shard_map/reduce_scatter | solution.py:22
  209.0 0.0 copy-done
  209.0 4.9 %fusion.2 = (bf16[128,6144]{1,0:T(8,128)(2,1)}, bf16[128,6144]{1,0:T(8,128)(2,1)}) fusion(bf16[128,6144]{1,0:T(8,128)(2,1)S(1)} %copy-done, f32[128,6144]{1,0:T(8,128)} %reduce-scatter.2.cloned.1.call-done), kind=kLoop, calls=%fused_computation.7 | loop fusion | flops 18087936 | bytes 7864320 | tf_op jit(solution)/shard_map/convert_element_type | solution.py:25
  213.9 0.0 all-gather.5.cloned.1.call-update
  214.0 74.2 %all-gather.5.cloned.1.call-done = bf16[1024,6144]{1,0:T(8,128)(2,1)} async-done(((bf16[128,6144]{1,0:T(8,128)(2,1)}), bf16[1024,6144]{1,0:T(8,128)(2,1)}) %all-gather.5.cloned.1.call-update) | async-done | bytes 12582928 | tf_op jit(solution)/shard_map/all_gather | solution.py:29
  288.1 27.9 %convolution_convert_fusion = bf16[1536,6144]{1,0:T(8,128)(2,1)} fusion(bf16[1024,6144]{1,0:T(8,128)(2,1)} %all-gather.5.cloned.1.call-done, bf16[1024,6144]{1,0:T(8,128)(2,1)} %all-gather.3.cloned.1.call-done, s32[]{:T(128)S(6)} %select_n.7), kind=kOutput, calls=%fused_computation | convolution fusion | flops 19336790016 | bytes 34603012 | tf_op jit(solution)/shard_map/dot_general | solution.py:12
Async XLA Ops:
  7.2 157.8 %all-gather.3.cloned.1.call-start = ((), (), s32[]{:S(2)}) async-start(), calls=%async_computation.1 | async-start | bytes 13369344 | tf_op jit(solution)/shard_map/all_gather | solution.py:18
  7.9 201.1 %reduce-scatter.2.cloned.1.call-start = ((), (), s32[]{:S(2)}) async-start(), calls=%async_computation.2 | async-start | bytes 9437184 | tf_op jit(solution)/shard_map/reduce_scatter | solution.py:22
  196.6 12.4 %copy-start = (bf16[128,6144]{1,0:T(8,128)(2,1)S(1)}, bf16[128,6144]{1,0:T(8,128)(2,1)}, u32[]{:S(2)}) copy-start(bf16[128,6144]{1,0:T(8,128)(2,1)} %param.5) | copy-start | bytes 4718596
  196.6 91.5 %all-gather.5.cloned.1.call-start = ((), (), s32[]{:S(2)}) async-start(), calls=%async_computation.3 | async-start | bytes 14155776 | tf_op jit(solution)/shard_map/all_gather | solution.py:29
Sparse Core Ops, SparseCore 0:
  10.8 154.1 all-gather.2
  196.8 12.2 reduce-scatter.1
  214.1 73.9 all-gather.4
where the time goes:
time: 323 us
  waiting for transfers between devices  244 us (76%)
  matrix products  59.5 us (18%)
  between operations  13.8 us (4%)
  other arithmetic  4.9 us (2%)
    all_gather x1, waiting for transfers between devices, local(): all_rows = lax.all_gather(tokens, ('dp', 'depth'), axis=0, tiled=True)  157 us
    all_gather x1, waiting for transfers between devices, local(): lax.all_gather(grad_pre, ('dp', 'grid'), axis=0, tiled=True)  74.2 us
    dot_general x1, matrix products, local(): partial_pre = jnp.dot(own_rows, weight, preferred_element_type=jnp.float32)  31.6 us
    dot_general x1, matrix products, transposed_product(): lax.dot_general(left, right, (((0,), (0,)), ((), ())), preferred_element_...  27.9 us
    reduce_scatter x1, waiting for transfers between devices, local(): lax.psum_scatter(partial_pre, 'grid', scatter_dimension=0, tiled=True)  12.3 us
  transfers between devices with their start and end apart: 3, of which 3 were waited for; matrix products, arithmetic and copies ran while one was open for 0% of the time, Pallas kernels for 0%

commit v1 on v0

--- a/solution.py
+++ b/solution.py
@@ -1,7 +1,21 @@
+import functools
 import jax
 import jax.numpy as jnp
 from jax import lax
 from jax.sharding import PartitionSpec as P
+
+
+def masks_take(v0, named_axis, axis_no):
+    n_dev_all = lax.psum(1, axis_name=named_axis)
+    arrivals = []
+    for w in [*range(v0.ndim)]:
+        arrivals.append(n_dev_all if w == axis_no else 1)
+    return lax.all_to_all(
+        jnp.tile(v0, arrivals), named_axis, split_axis=axis_no, concat_axis=axis_no, tiled=True
+    )
+
+
+shape_members_all = functools.partial(masks_take, named_axis=("dp", "depth"), axis_no=0)
 
 
 def gelu_tanh(values):
@@ -15,7 +29,7 @@
 
 
 def local(tokens, weight, cotangent):
-    all_rows = lax.all_gather(tokens, ("dp", "depth"), axis=0, tiled=True)
+    all_rows = shape_members_all(tokens)
     group_size = all_rows.shape[0] // lax.axis_size("dp")
     own_rows = lax.dynamic_slice_in_dim(all_rows, lax.axis_index("dp") * group_size, group_size, 0)
     partial_pre = jnp.dot(own_rows, weight, preferred_element_type=jnp.float32)

time: 323 us -> 475 us (1.47)
  waiting for transfers between devices: 244 us -> 380 us
  starting transfers between devices: 0.12 us -> 8.65 us
  local copies, waits for them, and re-layouts: 0.01 us -> 7.54 us
    all_to_all x0 -> x1, waiting for transfers between devices: none -> 296 us  [masks_take(): lax.all_to_all(jnp.tile(v0, arrivals), named_axis, split_axis=axis_no, co...]
    all_gather x1 -> x0, waiting for transfers between devices: 157 us -> none  [local(): all_rows = lax.all_gather(tokens, ('dp', 'depth'), axis=0, tiled=True)]
    all_to_all x0 -> x1, starting transfers between devices: none -> 8.39 us  [masks_take(): lax.all_to_all(jnp.tile(v0, arrivals), named_axis, split_axis=axis_no, co...]
    another operation x0 -> x1, local copies, waits for them, and re-layouts: none -> 7.54 us  [masks_take(): jnp.tile(v0, arrivals)]
where the time goes in v1:
time: 475 us
  waiting for transfers between devices  380 us (80%)
  matrix products  59.5 us (13%)
  between operations  14.1 us (3%)
  starting transfers between devices  8.65 us (2%)
  local copies, waits for them, and re-layouts  7.54 us (2%)
  other arithmetic  4.9 us (1%)
    all_to_all x1, waiting for transfers between devices, masks_take(): lax.all_to_all(jnp.tile(v0, arrivals), named_axis, split_axis=axis_no, co...  296 us
    all_gather x1, waiting for transfers between devices, local(): lax.all_gather(grad_pre, ('dp', 'grid'), axis=0, tiled=True)  74.2 us
    dot_general x1, matrix products, local(): partial_pre = jnp.dot(own_rows, weight, preferred_element_type=jnp.float32)  31.6 us
    dot_general x1, matrix products, transposed_product(): lax.dot_general(left, right, (((0,), (0,)), ((), ())), preferred_element_...  27.9 us
    reduce_scatter x1, waiting for transfers between devices, local(): lax.psum_scatter(partial_pre, 'grid', scatter_dimension=0, tiled=True)  10.4 us
  transfers between devices with their start and end apart: 3, of which 3 were waited for; matrix products, arithmetic and copies ran while one was open for 0% of the time, Pallas kernels for 0%

profile of v1, /device:TPU:0, one launch (start us, length us, event | category | flops | bytes accessed | tf_op | source)
XLA Modules:
  0.0 474.8 jit_solution(2424387515481224075)
XLA Ops:
  7.2 7.5 %tile.2 = bf16[16,64,6144]{2,1,0:T(8,128)(2,1)} broadcast(bf16[64,6144]{1,0:T(8,128)(2,1)} %param.3), dimensions={1,2} | broadcast | bytes 13369344 | tf_op jit(solution)/shard_map/tile | solution.py:14
  14.7 8.4 %all-to-all-start = ((bf16[16,64,6144]{2,1,0:T(8,128)(2,1)}), bf16[16,64,6144]{2,1,0:T(8,128)(2,1)}, u32[]{:S(2)}, u32[]{:S(2)}) async-start(bf16[16,64,6144]{2,1,0:T(8,128)(2,1)} %tile.2), calls=%async_computation | async-start | bytes 25165824 | tf_op jit(solution)/shard_map/all_to_all | solution.py:13
  23.1 0.0 reduce-scatter.2.cloned.1.call-start
  23.1 295.6 %all-to-all-done = bf16[16,64,6144]{2,1,0:T(8,128)(2,1)} async-done(((bf16[16,64,6144]{2,1,0:T(8,128)(2,1)}), bf16[16,64,6144]{2,1,0:T(8,128)(2,1)}, u32[]{:S(2)}, u32[]{:S(2)}) %all-to-all-start) | async-done | bytes 12582944 | tf_op jit(solution)/shard_map/all_to_all | solution.py:13
  318.7 31.6 %fusion.11 = f32[256,6144]{1,0:T(8,128)} fusion(bf16[6144,6144]{1,0:T(8,128)(2,1)} %param.4, bf16[1024,6144]{1,0:T(8,128)(2,1)} %bitcast, s32[]{:T(128)S(6)} %select_n.6), kind=kOutput, calls=%fused_computation.17 | convolution fusion | flops 19327352832 | bytes 84934656 | tf_op jit(solution)/shard_map/dot_general | solution.py:35
  350.3 0.0 copy-start
  350.3 0.0 reduce-scatter.2.cloned.1.call-update
  350.3 0.2 all-gather.2.cloned.1.call-start
  350.6 10.4 %reduce-scatter.2.cloned.1.call-done = f32[128,6144]{1,0:T(8,128)} async-done(((f32[256,6144]{1,0:T(8,128)}), f32[128,6144]{1,0:T(8,128)}) %reduce-scatter.2.cloned.1.call-update) | async-done | bytes 3145744 | tf_op jit(solution)/shard_map/reduce_scatter | solution.py:36
  360.9 0.0 copy-done
  360.9 4.9 %fusion.2 = (bf16[128,6144]{1,0:T(8,128)(2,1)}, bf16[128,6144]{1,0:T(8,128)(2,1)}) fusion(bf16[128,6144]{1,0:T(8,128)(2,1)S(1)} %copy-done, f32[128,6144]{1,0:T(8,128)} %reduce-scatter.2.cloned.1.call-done), kind=kLoop, calls=%fused_computation.7 | loop fusion | flops 18087936 | bytes 7864320 | tf_op jit(solution)/shard_map/convert_element_type | solution.py:39
  365.8 0.0 all-gather.2.cloned.1.call-update
  365.9 74.2 %all-gather.2.cloned.1.call-done = bf16[1024,6144]{1,0:T(8,128)(2,1)} async-done(((bf16[128,6144]{1,0:T(8,128)(2,1)}), bf16[1024,6144]{1,0:T(8,128)(2,1)}) %all-gather.2.cloned.1.call-update) | async-done | bytes 12582928 | tf_op jit(solution)/shard_map/all_gather | solution.py:43
  440.1 27.9 %convolution_convert_fusion = bf16[1536,6144]{1,0:T(8,128)(2,1)} fusion(bf16[1024,6144]{1,0:T(8,128)(2,1)} %all-gather.2.cloned.1.call-done, bf16[1024,6144]{1,0:T(8,128)(2,1)} %bitcast, s32[]{:T(128)S(6)} %select_n.7), kind=kOutput, calls=%fused_computation | convolution fusion | flops 19336790016 | bytes 34603012 | tf_op jit(solution)/shard_map/dot_general | solution.py:26
Async XLA Ops:
  14.7 304.0 %all-to-all-start = ((bf16[16,64,6144]{2,1,0:T(8,128)(2,1)}), bf16[16,64,6144]{2,1,0:T(8,128)(2,1)}, u32[]{:S(2)}, u32[]{:S(2)}) async-start(bf16[16,64,6144]{2,1,0:T(8,128)(2,1)} %tile.2), calls=%async_computation | async-start | bytes 25165824 | tf_op jit(solution)/shard_map/all_to_all | solution.py:13
  23.1 337.8 %reduce-scatter.2.cloned.1.call-start = ((), (), s32[]{:S(2)}) async-start(), calls=%async_computation.2 | async-start | bytes 9437184 | tf_op jit(solution)/shard_map/reduce_scatter | solution.py:36
  350.3 10.6 %copy-start = (bf16[128,6144]{1,0:T(8,128)(2,1)S(1)}, bf16[128,6144]{1,0:T(8,128)(2,1)}, u32[]{:S(2)}) copy-start(bf16[128,6144]{1,0:T(8,128)(2,1)} %param.5) | copy-start | bytes 4718596
  350.3 89.7 %all-gather.2.cloned.1.call-start = ((), (), s32[]{:S(2)}) async-start(), calls=%async_computation.3 | async-start | bytes 14155776 | tf_op jit(solution)/shard_map/all_gather | solution.py:43
Sparse Core Ops, SparseCore 0:
  350.5 10.4 reduce-scatter.1
  366.0 74.0 all-gather.1

commit v2 on v0

--- a/solution.py
+++ b/solution.py
@@ -2,6 +2,14 @@
 import jax.numpy as jnp
 from jax import lax
 from jax.sharding import PartitionSpec as P
+from jax.lax import all_to_all, axis_size
+
+
+def _proceed_figure(group_axis, on_dim, local_x):
+    local_now = jnp.concatenate(
+        all_to_all(jnp.stack(axis_size(group_axis) * [local_x], axis=0), group_axis, 0, 0), on_dim
+    )
+    return local_now
 
 
 def gelu_tanh(values):
@@ -26,7 +34,7 @@
     sub_width = all_rows.shape[1] // lax.axis_size("dp")
     columns = lax.dynamic_slice_in_dim(all_rows, lax.axis_index("dp") * sub_width, sub_width, 1)
     weight_grad = transposed_product(
-        columns, lax.all_gather(grad_pre, ("dp", "grid"), axis=0, tiled=True)
+        columns, _proceed_figure(("dp", "grid"), on_dim=0, local_x=grad_pre)
     )
     return (hidden, weight_grad.astype(jnp.bfloat16))
 

time: 323 us -> 400 us (1.24)
  waiting for transfers between devices: 244 us -> 309 us
  local copies, waits for them, and re-layouts: 0.01 us -> 6.49 us
  starting transfers between devices: 0.12 us -> 5.62 us
    all_to_all x0 -> x1, waiting for transfers between devices: none -> 139 us  [_proceed_figure(): all_to_all(jnp.stack(axis_size(group_axis) * [local_x], axis=0), group_ax...]
    all_gather x1 -> x0, waiting for transfers between devices: 74.2 us -> none  [local(): lax.all_gather(grad_pre, ('dp', 'grid'), axis=0, tiled=True)]
    another operation x0 -> x1, local copies, waits for them, and re-layouts: none -> 6.49 us  [_proceed_figure(): jnp.stack(axis_size(group_axis) * [local_x], axis=0)]
    all_to_all x0 -> x1, starting transfers between devices: none -> 5.55 us  [_proceed_figure(): all_to_all(jnp.stack(axis_size(group_axis) * [local_x], axis=0), group_ax...]
where the time goes in v2:
time: 400 us; the launch traced here: 399 us
  waiting for transfers between devices  309 us (77%)
  matrix products  59.5 us (15%)
  between operations  14.1 us (4%)
  local copies, waits for them, and re-layouts  6.49 us (2%)
  starting transfers between devices  5.62 us (1%)
  other arithmetic  4.64 us (1%)
    all_gather x1, waiting for transfers between devices, local(): all_rows = lax.all_gather(tokens, ('dp', 'depth'), axis=0, tiled=True)  157 us
    all_to_all x1, waiting for transfers between devices, _proceed_figure(): all_to_all(jnp.stack(axis_size(group_axis) * [local_x], axis=0), group_ax...  139 us
    dot_general x1, matrix products, local(): partial_pre = jnp.dot(own_rows, weight, preferred_element_type=jnp.float32)  31.6 us
    dot_general x1, matrix products, transposed_product(): lax.dot_general(left, right, (((0,), (0,)), ((), ())), preferred_element_...  27.9 us
    reduce_scatter x1, waiting for transfers between devices, local(): lax.psum_scatter(partial_pre, 'grid', scatter_dimension=0, tiled=True)  12.4 us
  transfers between devices with their start and end apart: 3, of which 3 were waited for; matrix products, arithmetic and copies ran while one was open for 0% of the time, Pallas kernels for 0%

profile of v2, /device:TPU:0, one launch (start us, length us, event | category | flops | bytes accessed | tf_op | source)
XLA Modules:
  0.0 399.3 jit_solution(507528476470847802)
XLA Ops:
  7.2 0.0 all-gather.2.cloned.1.call-start
  7.2 0.7 all-gather.2.cloned.1.call-update
  7.9 0.0 reduce-scatter.2.cloned.1.call-start
  7.9 157.1 %all-gather.2.cloned.1.call-done = bf16[1024,6144]{1,0:T(8,128)(2,1)} async-done(((bf16[64,6144]{1,0:T(8,128)(2,1)}), bf16[1024,6144]{1,0:T(8,128)(2,1)}) %all-gather.2.cloned.1.call-update) | async-done | bytes 12582928 | tf_op jit(solution)/shard_map/all_gather | solution.py:26
  165.0 31.6 %fusion.11 = f32[256,6144]{1,0:T(8,128)} fusion(bf16[6144,6144]{1,0:T(8,128)(2,1)} %param.4, bf16[1024,6144]{1,0:T(8,128)(2,1)} %all-gather.2.cloned.1.call-done, s32[]{:T(128)S(6)} %select_n.6), kind=kOutput, calls=%fused_computation.17 | convolution fusion | flops 19327352832 | bytes 84934656 | tf_op jit(solution)/shard_map/dot_general | solution.py:29
  196.6 0.0 copy-start
  196.6 0.0 reduce-scatter.2.cloned.1.call-update
  196.6 12.4 %reduce-scatter.2.cloned.1.call-done = f32[128,6144]{1,0:T(8,128)} async-done(((f32[256,6144]{1,0:T(8,128)}), f32[128,6144]{1,0:T(8,128)}) %reduce-scatter.2.cloned.1.call-update) | async-done | bytes 3145744 | tf_op jit(solution)/shard_map/reduce_scatter | solution.py:30
  209.0 0.0 copy-done
  209.0 4.6 %fusion.2 = (bf16[128,6144]{1,0:T(8,128)(2,1)S(1)}, bf16[128,6144]{1,0:T(8,128)(2,1)}) fusion(bf16[128,6144]{1,0:T(8,128)(2,1)S(1)} %copy-done, f32[128,6144]{1,0:T(8,128)} %reduce-scatter.2.cloned.1.call-done), kind=kLoop, calls=%fused_computation.7 | loop fusion | flops 18087936 | bytes 7864320 | tf_op jit(solution)/shard_map/convert_element_type | solution.py:33
  213.7 6.5 %stack.2 = bf16[8,128,6144]{2,1,0:T(8,128)(2,1)} broadcast(bf16[128,6144]{1,0:T(8,128)(2,1)S(1)} %get-tuple-element.2), dimensions={1,2} | broadcast | bytes 14155776 | tf_op jit(solution)/shard_map/stack | solution.py:10
  220.2 5.5 %all-to-all-start = ((bf16[8,128,6144]{2,1,0:T(8,128)(2,1)}), bf16[8,128,6144]{2,1,0:T(8,128)(2,1)}, u32[]{:S(2)}, u32[]{:S(2)}) async-start(bf16[8,128,6144]{2,1,0:T(8,128)(2,1)} %stack.2), calls=%async_computation.1 | async-start | bytes 25165824 | tf_op jit(solution)/shard_map/all_to_all | solution.py:10
  225.7 138.8 %all-to-all-done = bf16[8,128,6144]{2,1,0:T(8,128)(2,1)} async-done(((bf16[8,128,6144]{2,1,0:T(8,128)(2,1)}), bf16[8,128,6144]{2,1,0:T(8,128)(2,1)}, u32[]{:S(2)}, u32[]{:S(2)}) %all-to-all-start) | async-done | bytes 12582944 | tf_op jit(solution)/shard_map/all_to_all | solution.py:10
  364.6 27.9 %convolution_convert_fusion = bf16[1536,6144]{1,0:T(8,128)(2,1)} fusion(bf16[1024,6144]{1,0:T(8,128)(2,1)} %bitcast, bf16[1024,6144]{1,0:T(8,128)(2,1)} %all-gather.2.cloned.1.call-done, s32[]{:T(128)S(6)} %select_n.7), kind=kOutput, calls=%fused_computation | convolution fusion | flops 19336790016 | bytes 34603012 | tf_op jit(solution)/shard_map/dot_general | solution.py:20
Async XLA Ops:
  7.2 157.8 %all-gather.2.cloned.1.call-start = ((), (), s32[]{:S(2)}) async-start(), calls=%async_computation.2 | async-start | bytes 13369344 | tf_op jit(solution)/shard_map/all_gather | solution.py:26
  7.9 201.1 %reduce-scatter.2.cloned.1.call-start = ((), (), s32[]{:S(2)}) async-start(), calls=%async_computation.3 | async-start | bytes 9437184 | tf_op jit(solution)/shard_map/reduce_scatter | solution.py:30
  196.6 12.4 %copy-start = (bf16[128,6144]{1,0:T(8,128)(2,1)S(1)}, bf16[128,6144]{1,0:T(8,128)(2,1)}, u32[]{:S(2)}) copy-start(bf16[128,6144]{1,0:T(8,128)(2,1)} %param.5) | copy-start | bytes 4718596
  220.2 144.4 %all-to-all-start = ((bf16[8,128,6144]{2,1,0:T(8,128)(2,1)}), bf16[8,128,6144]{2,1,0:T(8,128)(2,1)}, u32[]{:S(2)}, u32[]{:S(2)}) async-start(bf16[8,128,6144]{2,1,0:T(8,128)(2,1)} %stack.2), calls=%async_computation.1 | async-start | bytes 25165824 | tf_op jit(solution)/shard_map/all_to_all | solution.py:10
Sparse Core Ops, SparseCore 0:
  10.8 154.1 all-gather.1
  196.8 12.2 reduce-scatter.1
